TPU v7x, 32 devices: a whole 2x2x4 slice. The times are simulated.
32 devices in a mesh: dp: 4 (over x, core), expert: 8 (over z, y).
Axes of the slice: x: 2, y: 2, z: 4, core: 2. Of those that a mesh axis runs over, the one named last changes fastest.
Arguments:
- tokens: bfloat16 [4096, 4096], P(('dp', 'expert')), may hold values from -6 to 6
- expert_ids: int32 [4096, 2], P(('dp', 'expert')), may hold values from 0 to 7, as said below
- gate_codes: int32 [4096, 2], P(('dp', 'expert')), may hold values from 1 to 64
- w_gate: bfloat16 [8, 4096, 768], P('expert'), may hold values from -0.09375 to 0.09375
- w_up: bfloat16 [8, 4096, 768], P('expert'), may hold values from -0.09375 to 0.09375
- w_down: bfloat16 [8, 768, 4096], P('expert'), may hold values from -0.21875 to 0.21875
- out_grad: bfloat16 [4096, 4096], P(('dp', 'expert')), may hold values from -6 to 6
Outputs:
- layer_out: bfloat16 [4096, 4096], P(('dp', 'expert'))
- tokens_grad: bfloat16 [4096, 4096], P(('dp', 'expert'))
- gate_weight_grad: bfloat16 [8, 4096, 768], P('expert', 'dp')
- up_weight_grad: bfloat16 [8, 4096, 768], P('expert', 'dp')
- down_weight_grad: bfloat16 [8, 768, 4096], P('expert', None, 'dp')
Inputs may be any that keep to these rules, and one draw needn't show every extreme that they name: `expert_ids`: each token names 2 different experts. In the rows of one device no expert is named more than 48 times, and in every draw one and the same expert is named exactly 48 times by the rows of every device.
All inputs are finite; a program needn't handle non-finite values.
Results may differ from a plain program's by a relative error of at most 0.009.
Values may be sent and summed in bfloat16 or wider, within the bound.
A program may use at most 192 MiB of HBM per device.

v0:
```python
import jax
import jax.numpy as jnp
from jax import lax
from jax.sharding import PartitionSpec as P


def slot_targets(block_ids, experts, capacity):
    flat_ids = block_ids.reshape(-1)
    one_hot = (flat_ids[:, None] == jnp.arange(experts, dtype=jnp.int32)[None, :]).astype(jnp.int32)
    earlier = jnp.cumsum(one_hot, axis=0) - one_hot
    slot_ranks = jnp.sum(earlier * one_hot, axis=1)
    return flat_ids * capacity + slot_ranks


def per_device(tokens, expert_ids, gate_codes, w_gate, w_up, w_down, out_grad):
    experts = lax.axis_size("expert")
    tok_count, model_width = tokens.shape
    top_count = expert_ids.shape[1]
    pair_count = tok_count * top_count
    capacity = 3 * pair_count // (2 * experts)
    targets = slot_targets(expert_ids, experts, capacity)
    owners = (
        jnp.full((experts * capacity,), -1, jnp.int32)
        .at[targets]
        .set(jnp.arange(pair_count, dtype=jnp.int32))
    )
    is_live = owners >= 0
    safe_pair = jnp.maximum(owners, 0)
    token_pos = safe_pair // top_count
    gate_flat = gate_codes.astype(jnp.float32).reshape(-1) / 64.0
    pair_gains = jnp.where(is_live, gate_flat[safe_pair], 0.0)
    outbound = jnp.where(is_live[:, None], tokens[token_pos], jnp.zeros((), jnp.bfloat16))
    outbound = outbound.reshape(experts, capacity, model_width)
    gate_matrix = w_gate[0]
    up_matrix = w_up[0]
    down_matrix = w_down[0]
    hidden_units = gate_matrix.shape[1]
    contract = (((1,), (1,)), ((), ()))
    contract_rows = (((0,), (0,)), ((), ()))
    received = lax.all_to_all(outbound, "expert", split_axis=0, concat_axis=0, tiled=True)
    slot_count = received.shape[1]
    expert_row_block = received.reshape(-1, model_width)
    pre_gate = jnp.dot(expert_row_block, gate_matrix, preferred_element_type=jnp.float32)
    pre_up = jnp.dot(expert_row_block, up_matrix, preferred_element_type=jnp.float32)
    expert_hidden = (pre_gate * jax.nn.sigmoid(pre_gate) * pre_up).astype(jnp.bfloat16)
    produced = jnp.dot(expert_hidden, down_matrix, preferred_element_type=jnp.float32).astype(
        jnp.bfloat16
    )
    produced = produced.reshape(experts, slot_count, model_width)
    returned = lax.all_to_all(produced, "expert", split_axis=0, concat_axis=0, tiled=True)
    returned, arrived, pre_gate, pre_up, hidden = (
        returned,
        received,
        pre_gate.reshape(experts, slot_count, hidden_units),
        pre_up.reshape(experts, slot_count, hidden_units),
        expert_hidden.reshape(experts, slot_count, hidden_units),
    )
    pair_out = returned.reshape(-1, model_width)[targets].astype(jnp.float32)
    weighted = gate_flat[:, None] * pair_out
    layer_out = jnp.sum(weighted.reshape(tok_count, top_count, model_width), axis=1).astype(
        jnp.bfloat16
    )
    upstream = out_grad[token_pos]
    pair_grad = (pair_gains[:, None] * upstream.astype(jnp.float32)).astype(jnp.bfloat16)
    pair_grad = pair_grad.reshape(experts, capacity, model_width)
    incoming = lax.all_to_all(pair_grad, "expert", split_axis=0, concat_axis=0, tiled=True).reshape(
        -1, model_width
    )
    pre_gate = pre_gate.reshape(-1, hidden_units)
    pre_up = pre_up.reshape(-1, hidden_units)
    hidden = hidden.reshape(-1, hidden_units)
    sigmoid_gate = jax.nn.sigmoid(pre_gate)
    silu_gate = pre_gate * sigmoid_gate
    hidden_grad = lax.dot_general(
        incoming, down_matrix, contract, preferred_element_type=jnp.float32
    )
    gate_pre_grad = (
        hidden_grad * pre_up * sigmoid_gate * (1.0 + pre_gate * (1.0 - sigmoid_gate))
    ).astype(jnp.bfloat16)
    up_pre_grad = (hidden_grad * silu_gate).astype(jnp.bfloat16)
    input_grad = lax.dot_general(
        gate_pre_grad, gate_matrix, contract, preferred_element_type=jnp.float32
    )
    input_grad = input_grad + lax.dot_general(
        up_pre_grad, up_matrix, contract, preferred_element_type=jnp.float32
    )
    input_grad = input_grad.astype(jnp.bfloat16).reshape(experts, capacity, model_width)
    returned_grad = lax.all_to_all(input_grad, "expert", split_axis=0, concat_axis=0, tiled=True)
    pair_input = returned_grad.reshape(-1, model_width)[targets].astype(jnp.float32)
    tokens_grad = jnp.sum(pair_input.reshape(tok_count, top_count, model_width), axis=1).astype(
        jnp.bfloat16
    )
    row_block = arrived.reshape(-1, model_width)
    column_block = row_block
    gate_sum = lax.psum_scatter(
        lax.dot_general(
            column_block, gate_pre_grad, contract_rows, preferred_element_type=jnp.float32
        ).astype(jnp.bfloat16),
        "dp",
        scatter_dimension=0,
        tiled=True,
    )
    column_block = row_block
    up_sum = lax.psum_scatter(
        lax.dot_general(
            column_block, up_pre_grad, contract_rows, preferred_element_type=jnp.float32
        ).astype(jnp.bfloat16),
        "dp",
        scatter_dimension=0,
        tiled=True,
    )
    column_block = incoming
    down_sum = (
        lax.psum_scatter(
            lax.dot_general(
                column_block, hidden, contract_rows, preferred_element_type=jnp.float32
            ).astype(jnp.bfloat16),
            "dp",
            scatter_dimension=0,
            tiled=True,
        )
        .astype(jnp.float32)
        .T
    )
    return (
        layer_out,
        tokens_grad,
        gate_sum[None],
        up_sum[None],
        down_sum.astype(jnp.bfloat16)[None],
    )


def solution(mesh):
    placed = (
        P(("dp", "expert"), None),
        P(("dp", "expert"), None),
        P(("dp", "expert"), None),
        P("expert", None, None),
        P("expert", None, None),
        P("expert", None, None),
        P(("dp", "expert"), None),
    )
    return jax.shard_map(
        per_device,
        mesh=mesh,
        in_specs=placed,
        out_specs=(
            P(("dp", "expert"), None),
            P(("dp", "expert"), None),
            P("expert", "dp", None),
            P("expert", "dp", None),
            P("expert", None, "dp"),
        ),
        check_vma=False,
    )
```

profile of v0, /device:TPU:0, one launch (start us, length us, event | category | flops | bytes accessed | tf_op | source)
XLA Modules:
  0.0 404.6 jit_solution(15272280271444568787)
XLA Ops:
  11.2 1.4 scatter_custom_fusion
  12.6 2.8 gather_fusion.2
  15.5 4.1 %gather_fusion.3 = bf16[384,4096]{1,0:T(8,128)(2,1)} fusion(bf16[128,4096]{1,0:T(8,128)(2,1)S(1)} %copy-done, s32[1024]{0:T(1024)S(1)} %get-tuple-element.23), kind=kCustom, calls=%fused_computation.3 | custom fusion | bytes 6292992 | tf_op jit(solution)/shard_map/gather | solution.py:63
  19.6 4.6 %fusion = bf16[8,48,4096]{2,1,0:T(8,128)(2,1)} fusion(bf16[8,48,4096]{2,1,0:T(8,128)(2,1)} %bitcast.60, f32[8,48]{1,0:T(8,128)S(1)} %mul.69), kind=kLoop, calls=%fused_computation.10 | loop fusion | flops 4718592 | bytes 6292992 | tf_op jit(solution)/shard_map/convert_element_type | solution.py:64
  24.2 7.4 %all-to-all-start.2 = ((bf16[8,48,4096]{2,1,0:T(8,128)(2,1)}), bf16[8,48,4096]{2,1,0:T(8,128)(2,1)}, u32[]{:S(2)}, u32[]{:S(2)}) async-start(bf16[8,48,4096]{2,1,0:T(8,128)(2,1)} %fusion), calls=%async_computation.2 | async-start | bytes 6291456 | tf_op jit(solution)/shard_map/all_to_all | solution.py:66
  31.7 4.0 gather_fusion
  35.7 3.9 broadcast_select_fusion
  39.6 62.8 %all-to-all-done.2 = bf16[8,48,4096]{2,1,0:T(8,128)(2,1)} async-done(((bf16[8,48,4096]{2,1,0:T(8,128)(2,1)}), bf16[8,48,4096]{2,1,0:T(8,128)(2,1)}, u32[]{:S(2)}, u32[]{:S(2)}) %all-to-all-start.2) | async-done | bytes 3145760 | tf_op jit(solution)/shard_map/all_to_all | solution.py:66
  102.4 3.6 all-to-all-start
  106.6 7.4 %fusion.1 = f32[384,768]{1,0:T(8,128)} fusion(bf16[384,4096]{1,0:T(8,128)(2,1)} %bitcast.12, bf16[1,768,4096]{2,1,0:T(8,128)(2,1)} %param.12), kind=kOutput, calls=%fused_computation.11 | convolution fusion | flops 2415919104 | bytes 10616832 | tf_op jit(solution)/shard_map/dot_general | solution.py:74
  114.0 63.0 %all-to-all-done = bf16[8,48,4096]{2,1,0:T(8,128)(2,1)S(1)} async-done(((bf16[8,48,4096]{2,1,0:T(8,128)(2,1)}), bf16[8,48,4096]{2,1,0:T(8,128)(2,1)S(1)}, u32[]{:S(2)}, u32[]{:S(2)}) %all-to-all-start) | async-done | bytes 3145760 | tf_op jit(solution)/shard_map/all_to_all | solution.py:40
  176.9 5.5 %fusion.7 = f32[384,768]{1,0:T(8,128)S(1)} fusion(bf16[384,4096]{1,0:T(8,128)(2,1)S(1)} %bitcast.61, bf16[1,4096,768]{2,1,0:T(8,128)(2,1)} %param.11), kind=kOutput, calls=%fused_computation.17 | convolution fusion | flops 2415919104 | bytes 10616832 | tf_op jit(solution)/shard_map/dot_general | solution.py:44
  182.4 6.8 %multiply_convert_fusion.1 = (bf16[384,768]{1,0:T(8,128)(2,1)}, bf16[384,768]{1,0:T(8,128)(2,1)}, bf16[384,768]{1,0:T(8,128)(2,1)S(1)}) fusion(f32[384,768]{1,0:T(8,128)S(1)} %copy-done.6, f32[384,768]{1,0:T(8,128)S(1)} %fusion.7, bf16[384,4096]{1,0:T(8,128)(2,1)S(1)} %bitcast.62, bf16[1,4096,768]{2,1,0:T(8,128)(2,1)} %param.10), kind=kOutput, calls=%fused_computation.28 | convolution fusion | flops 2420342784 | bytes 13565952 | tf_op jit(solution)/shard_map/dot_general | solution.py:43
  189.2 0.8 copy-done.4
  190.0 8.0 %convolution_convert_fusion = bf16[4096,768]{1,0:T(8,128)(2,1)} fusion(bf16[384,4096]{1,0:T(8,128)(2,1)} %bitcast.12, bf16[384,768]{1,0:T(8,128)(2,1)S(1)} %get-tuple-element.19), kind=kOutput, calls=%fused_computation.6 | convolution fusion | flops 2419064832 | bytes 10027008 | tf_op jit(solution)/shard_map/dot_general | solution.py:115
  198.1 6.4 %convolution_convert_fusion.2 = bf16[4096,768]{1,0:T(8,128)(2,1)} fusion(bf16[384,4096]{1,0:T(8,128)(2,1)S(1)} %bitcast.63, bf16[384,768]{1,0:T(8,128)(2,1)} %get-tuple-element.17), kind=kOutput, calls=%fused_computation.8 | convolution fusion | flops 2419064832 | bytes 10027008 | tf_op jit(solution)/shard_map/dot_general | solution.py:96
  204.8 6.7 %convolution_convert_fusion.1 = bf16[4096,768]{1,0:T(8,128)(2,1)} fusion(bf16[384,4096]{1,0:T(8,128)(2,1)S(1)} %bitcast.64, bf16[384,768]{1,0:T(8,128)(2,1)} %get-tuple-element.18), kind=kOutput, calls=%fused_computation.7 | convolution fusion | flops 2419064832 | bytes 10027008 | tf_op jit(solution)/shard_map/dot_general | solution.py:105
  211.5 1.0 copy-done.5
  212.5 6.8 %fusion.15 = bf16[384,4096]{1,0:T(8,128)(2,1)} fusion(bf16[384,768]{1,0:T(8,128)(2,1)S(1)} %copy-done.5, bf16[1,768,4096]{2,1,0:T(8,128)(2,1)} %param.12), kind=kOutput, calls=%fused_computation.24 | convolution fusion | flops 2417491968 | bytes 10027008 | tf_op jit(solution)/shard_map/dot_general | solution.py:46
  219.3 3.7 all-to-all-start.1
  223.0 4.9 %fusion.5 = f32[384,4096]{1,0:T(8,128)S(1)} fusion(bf16[384,768]{1,0:T(8,128)(2,1)} %get-tuple-element.18, bf16[1,4096,768]{2,1,0:T(8,128)(2,1)} %param.11), kind=kOutput, calls=%fused_computation.15 | convolution fusion | flops 2415919104 | bytes 13172736 | tf_op jit(solution)/shard_map/dot_general | solution.py:84
  227.9 8.5 %add_convert_fusion = bf16[384,4096]{1,0:T(8,128)(2,1)} fusion(f32[384,4096]{1,0:T(8,128)S(1)} %fusion.5, bf16[384,768]{1,0:T(8,128)(2,1)S(1)} %copy-done.3, bf16[1,4096,768]{2,1,0:T(8,128)(2,1)} %param.10), kind=kOutput, calls=%fused_computation.23 | convolution fusion | flops 2419064832 | bytes 16318464 | tf_op jit(solution)/shard_map/dot_general | solution.py:81
  236.5 57.5 %all-to-all-done.1 = bf16[8,48,4096]{2,1,0:T(8,128)(2,1)S(1)} async-done(((bf16[8,48,4096]{2,1,0:T(8,128)(2,1)}), bf16[8,48,4096]{2,1,0:T(8,128)(2,1)S(1)}, u32[]{:S(2)}, u32[]{:S(2)}) %all-to-all-start.1) | async-done | bytes 3145760 | tf_op jit(solution)/shard_map/all_to_all | solution.py:50
  294.0 4.4 %all-to-all-start.3 = ((bf16[8,48,4096]{2,1,0:T(8,128)(2,1)}), bf16[8,48,4096]{2,1,0:T(8,128)(2,1)}, u32[]{:S(2)}, u32[]{:S(2)}) async-start(bf16[8,48,4096]{2,1,0:T(8,128)(2,1)} %bitcast.65), calls=%async_computation.3 | async-start | bytes 6291456 | tf_op jit(solution)/shard_map/all_to_all | solution.py:88
  298.4 3.2 gather_fusion.1
  301.6 5.5 %reshape.118 = f32[128,2,4096]{2,1,0:T(2,128)} reshape(bf16[256,4096]{1,0:T(8,128)(2,1)} %gather_fusion.1) | data formatting | bytes 6291456 | tf_op jit(solution)/shard_map/convert_element_type | solution.py:58
  307.1 61.5 %all-to-all-done.3 = bf16[8,48,4096]{2,1,0:T(8,128)(2,1)} async-done(((bf16[8,48,4096]{2,1,0:T(8,128)(2,1)}), bf16[8,48,4096]{2,1,0:T(8,128)(2,1)}, u32[]{:S(2)}, u32[]{:S(2)}) %all-to-all-start.3) | async-done | bytes 3145760 | tf_op jit(solution)/shard_map/all_to_all | solution.py:88
  368.6 6.2 %gather_fusion.4 = bf16[256,4096]{1,0:T(8,128)(2,1)S(1)} fusion(bf16[384,4096]{1,0:T(8,128)(2,1)} %bitcast.14, s32[1024]{0:T(1024)S(1)} %pad_clamp_fusion.1), kind=kCustom, calls=%fused_computation.4 | custom fusion | bytes 4195328 | tf_op jit(solution)/shard_map/gather | solution.py:89
  374.8 2.9 gather.25
  377.7 7.9 %reduce_sum.35 = bf16[128,4096]{1,0:T(8,128)(2,1)} reduce(bf16[128,2,4096]{2,1,0:T(2,128)(2,1)} %gather.25, bf16[]{:T(256)} %constant.39.clone.1), dimensions={1}, to_apply=%region_5.6 | reduce | flops 524288 | bytes 3145730 | tf_op jit(solution)/shard_map/reduce_sum | solution.py:90
  385.6 9.6 %multiply_reduce_fusion = bf16[128,4096]{1,0:T(8,128)(2,1)} fusion(f32[128,2,4096]{2,1,0:T(2,128)} %reshape.118, f32[128,2]{1,0:T(8,128)S(1)} %copy.14), kind=kLoop, calls=%fused_computation.25 | loop fusion | flops 1572864 | bytes 5243904 | tf_op jit(solution)/shard_map/reduce_sum | solution.py:60
  395.2 2.6 copy.19
  (44 shorter events, 5.0 us)
Async XLA Ops:
  7.2 8.4 %copy-start = (bf16[128,4096]{1,0:T(8,128)(2,1)S(1)}, bf16[128,4096]{1,0:T(8,128)(2,1)}, u32[]{:S(2)}) copy-start(bf16[128,4096]{1,0:T(8,128)(2,1)} %param.13) | copy-start | bytes 3145732
  24.2 7.5 %copy-start.2 = (bf16[128,4096]{1,0:T(8,128)(2,1)S(1)}, bf16[128,4096]{1,0:T(8,128)(2,1)}, u32[]{:S(2)}) copy-start(bf16[128,4096]{1,0:T(8,128)(2,1)} %param.7) | copy-start | bytes 3145732
  24.2 78.2 %all-to-all-start.2 = ((bf16[8,48,4096]{2,1,0:T(8,128)(2,1)}), bf16[8,48,4096]{2,1,0:T(8,128)(2,1)}, u32[]{:S(2)}, u32[]{:S(2)}) async-start(bf16[8,48,4096]{2,1,0:T(8,128)(2,1)} %fusion), calls=%async_computation.2 | async-start | bytes 6291456 | tf_op jit(solution)/shard_map/all_to_all | solution.py:66
  102.4 74.5 %all-to-all-start = ((bf16[8,48,4096]{2,1,0:T(8,128)(2,1)}), bf16[8,48,4096]{2,1,0:T(8,128)(2,1)S(1)}, u32[]{:S(2)}, u32[]{:S(2)}) async-start(bf16[8,48,4096]{2,1,0:T(8,128)(2,1)} %broadcast_select_fusion), calls=%async_computation | async-start | bytes 6291456 | tf_op jit(solution)/shard_map/all_to_all | solution.py:40
  106.1 289.1 %reduce-scatter.8.cloned.1.call-start = ((), (), s32[]{:S(2)}) async-start(), calls=%async_computation.9 | async-start | bytes 7864320 | tf_op jit(solution)/shard_map/reduce_scatter | solution.py:114
  176.9 5.5 %copy-start.6 = (f32[384,768]{1,0:T(8,128)S(1)}, f32[384,768]{1,0:T(8,128)}, u32[]{:S(2)}) copy-start(f32[384,768]{1,0:T(8,128)} %fusion.1) | copy-start | bytes 3538948
  189.2 0.8 copy-start.4
  198.1 199.7 %reduce-scatter.4.cloned.1.call-start = ((), (), s32[]{:S(2)}) async-start(), calls=%async_computation.7 | async-start | bytes 7864320 | tf_op jit(solution)/shard_map/reduce_scatter | solution.py:95
  204.6 193.2 %reduce-scatter.6.cloned.1.call-start = ((), (), s32[]{:S(2)}) async-start(), calls=%async_computation.8 | async-start | bytes 7864320 | tf_op jit(solution)/shard_map/reduce_scatter | solution.py:104
  211.4 1.1 copy-start.5
  219.3 74.7 %all-to-all-start.1 = ((bf16[8,48,4096]{2,1,0:T(8,128)(2,1)}), bf16[8,48,4096]{2,1,0:T(8,128)(2,1)S(1)}, u32[]{:S(2)}, u32[]{:S(2)}) async-start(bf16[8,48,4096]{2,1,0:T(8,128)(2,1)} %bitcast.66), calls=%async_computation.1 | async-start | bytes 6291456 | tf_op jit(solution)/shard_map/all_to_all | solution.py:50
  223.0 5.0 %copy-start.3 = (bf16[384,768]{1,0:T(8,128)(2,1)S(1)}, bf16[384,768]{1,0:T(8,128)(2,1)}, u32[]{:S(2)}) copy-start(bf16[384,768]{1,0:T(8,128)(2,1)} %get-tuple-element.17) | copy-start | bytes 1769476
  294.0 74.6 %all-to-all-start.3 = ((bf16[8,48,4096]{2,1,0:T(8,128)(2,1)}), bf16[8,48,4096]{2,1,0:T(8,128)(2,1)}, u32[]{:S(2)}, u32[]{:S(2)}) async-start(bf16[8,48,4096]{2,1,0:T(8,128)(2,1)} %bitcast.65), calls=%async_computation.3 | async-start | bytes 6291456 | tf_op jit(solution)/shard_map/all_to_all | solution.py:88
  377.7 20.1 %copy-start.1 = (bf16[128,4096]{1,0:T(8,128)(2,1)S(1)}, bf16[128,4096]{1,0:T(8,128)(2,1)}, u32[]{:S(2)}) copy-start(bf16[128,4096]{1,0:T(8,128)(2,1)} %param.13) | copy-start | bytes 3145732
Sparse Core Ops, SparseCore 0:
  198.2 57.3 reduce-scatter.7
  258.9 58.3 reduce-scatter.3
  320.4 58.3 reduce-scatter.5
where the time goes:
time: 410 us; the launch traced here: 405 us
  waiting for transfers between devices  245 us (60%)
  matrix products  61 us (15%)
  local copies, waits for them, and re-layouts  36.4 us (9%)
  other arithmetic  28.2 us (7%)
  starting transfers between devices  20 us (5%)
  between operations  14.2 us (3%)
    all_to_all x1, waiting for transfers between devices, per_device(): lax.all_to_all(outbound, 'expert', split_axis=0, concat_axis=0, tiled=True)  63 us
    all_to_all x1, waiting for transfers between devices, per_device(): lax.all_to_all(pair_grad, 'expert', split_axis=0, concat_axis=0, tiled=True)  62.8 us
    all_to_all x1, waiting for transfers between devices, per_device(): lax.all_to_all(input_grad, 'expert', split_axis=0, concat_axis=0, tiled=T...  61.5 us
    all_to_all x1, waiting for transfers between devices, per_device(): lax.all_to_all(produced, 'expert', split_axis=0, concat_axis=0, tiled=True)  57.5 us
    reduce_sum x1, other arithmetic, per_device(): jnp.sum(weighted.reshape(tok_count, top_count, model_width), axis=1)  9.64 us
    gather x2, local copies, waits for them, and re-layouts, per_device(): returned_grad.reshape(-1, model_width)[targets].astype(jnp.float32)  9.04 us
    dot_general x1, matrix products, per_device(): lax.dot_general(gate_pre_grad, gate_matrix, contract, preferred_element_t...  8.54 us
  transfers between devices with their start and end apart: 7, of which 4 were waited for; matrix products, arithmetic and copies ran while one was open for 21% of the time, Pallas kernels for 0%

commit v1 on v0

--- a/solution.py
+++ b/solution.py
@@ -2,6 +2,17 @@
 import jax.numpy as jnp
 from jax import lax
 from jax.sharding import PartitionSpec as P
+
+
+def use_fields_here(here_x, out_dim, my_data):
+    x_next, big = (here_x.shape[:out_dim], here_x.shape[out_dim + 1 :])
+    return jnp.moveaxis(here_x.reshape(*x_next, my_data, -1, *big), out_dim, 0)
+
+
+def joints_remake(x_in, d_out):
+    x_in = jnp.moveaxis(x_in, 0, d_out)
+    f_next = x_in.shape
+    return x_in.reshape(*f_next[:d_out], f_next[d_out] * f_next[d_out + 1], *f_next[d_out + 2 :])
 
 
 def slot_targets(block_ids, experts, capacity):
@@ -85,7 +96,16 @@
         up_pre_grad, up_matrix, contract, preferred_element_type=jnp.float32
     )
     input_grad = input_grad.astype(jnp.bfloat16).reshape(experts, capacity, model_width)
-    returned_grad = lax.all_to_all(input_grad, "expert", split_axis=0, concat_axis=0, tiled=True)
+    last, a_next = (lax.axis_size("expert"), lax.axis_index("expert"))
+    block_next = use_fields_here(input_grad, 0, last)
+    frames = [block_next[a_next]]
+    for j in range(1, last):
+        w_next = block_next[a_next ^ j]
+        frames.append(
+            lax.ppermute(w_next, axis_name="expert", perm=[(no, no ^ j) for no in range(last)])
+        )
+    block_next = jnp.stack(frames, 0)[a_next ^ jnp.arange(last)]
+    returned_grad = joints_remake(block_next, 0)
     pair_input = returned_grad.reshape(-1, model_width)[targets].astype(jnp.float32)
     tokens_grad = jnp.sum(pair_input.reshape(tok_count, top_count, model_width), axis=1).astype(
         jnp.bfloat16

time: 410 us -> 450 us (1.098)
  starting transfers between devices: 20 us -> 41.4 us
  local copies, waits for them, and re-layouts: 36.4 us -> 52 us
  waiting for transfers between devices: 245 us -> 250 us
    ppermute x0 -> x7, waiting for transfers between devices: none -> 124 us  [per_device(): lax.ppermute(w_next, axis_name='expert', perm=[(no, no ^ j) for no in ran...]
    all_to_all x1 -> x0, waiting for transfers between devices: 61.5 us -> none  [per_device(): lax.all_to_all(input_grad, 'expert', split_axis=0, concat_axis=0, tiled=T...]
    all_to_all x1, waiting for transfers between devices: 57.5 us -> 0.01 us  [per_device(): lax.all_to_all(produced, 'expert', split_axis=0, concat_axis=0, tiled=True)]
    ppermute x0 -> x7, starting transfers between devices: none -> 13.8 us  [per_device(): lax.ppermute(w_next, axis_name='expert', perm=[(no, no ^ j) for no in ran...]
    reduce_scatter x1, starting transfers between devices: 0.21 us -> 12.3 us  [per_device(): lax.psum_scatter(lax.dot_general(column_block, up_pre_grad, contract_rows...]
    unnamed x16 -> x32, local copies, waits for them, and re-layouts: 5.24 us -> 10.9 us
  transfers between devices with their start and end apart: 7 -> 13, of which waited for: 4 -> 5; matrix products, arithmetic and copies ran while one was open for 21% -> 22% of each run, Pallas kernels for 0% -> 0%
where the time goes in v1:
time: 450 us; the launch traced here: 444 us
  waiting for transfers between devices  250 us (56%)
  matrix products  58.5 us (13%)
  local copies, waits for them, and re-layouts  52 us (12%)
  starting transfers between devices  41.4 us (9%)
  other arithmetic  27.9 us (6%)
  between operations  14.2 us (3%)
    ppermute x7, waiting for transfers between devices, per_device(): lax.ppermute(w_next, axis_name='expert', perm=[(no, no ^ j) for no in ran...  124 us
    all_to_all x1, waiting for transfers between devices, per_device(): lax.all_to_all(outbound, 'expert', split_axis=0, concat_axis=0, tiled=True)  63.1 us
    all_to_all x1, waiting for transfers between devices, per_device(): lax.all_to_all(pair_grad, 'expert', split_axis=0, concat_axis=0, tiled=True)  62.8 us
    ppermute x7, starting transfers between devices, per_device(): lax.ppermute(w_next, axis_name='expert', perm=[(no, no ^ j) for no in ran...  13.8 us
    reduce_scatter x1, starting transfers between devices, per_device(): lax.psum_scatter(lax.dot_general(column_block, up_pre_grad, contract_rows...  12.3 us
    gather x2, local copies, waits for them, and re-layouts, per_device(): returned_grad.reshape(-1, model_width)[targets].astype(jnp.float32)  12 us
    unnamed x32, local copies, waits for them, and re-layouts  10.9 us
    reduce_sum x1, other arithmetic, per_device(): jnp.sum(weighted.reshape(tok_count, top_count, model_width), axis=1)  9.64 us
  transfers between devices with their start and end apart: 13, of which 5 were waited for; matrix products, arithmetic and copies ran while one was open for 22% of the time, Pallas kernels for 0%

profile of v1, /device:TPU:0, one launch (start us, length us, event | category | flops | bytes accessed | tf_op | source)
XLA Modules:
  0.0 443.8 jit_solution(12038508680862612865)
XLA Ops:
  12.6 2.8 gather_fusion.2
  15.5 4.1 gather_fusion.3
  19.6 4.5 %fusion = bf16[8,48,4096]{2,1,0:T(8,128)(2,1)} fusion(bf16[8,48,4096]{2,1,0:T(8,128)(2,1)} %bitcast.92, f32[8,48]{1,0:T(8,128)S(1)} %mul.69), kind=kLoop, calls=%fused_computation.11 | loop fusion | flops 4718592 | bytes 6292992 | tf_op jit(solution)/shard_map/convert_element_type | solution.py:75
  24.1 7.4 %all-to-all-start.2 = ((bf16[8,48,4096]{2,1,0:T(8,128)(2,1)}), bf16[8,48,4096]{2,1,0:T(8,128)(2,1)}, u32[]{:S(2)}, u32[]{:S(2)}) async-start(bf16[8,48,4096]{2,1,0:T(8,128)(2,1)} %fusion), calls=%async_computation.2 | async-start | bytes 6291456 | tf_op jit(solution)/shard_map/all_to_all | solution.py:77
  31.6 4.1 gather_fusion
  35.7 3.8 broadcast_select_fusion
  39.5 62.8 %all-to-all-done.2 = bf16[8,48,4096]{2,1,0:T(8,128)(2,1)} async-done(((bf16[8,48,4096]{2,1,0:T(8,128)(2,1)}), bf16[8,48,4096]{2,1,0:T(8,128)(2,1)}, u32[]{:S(2)}, u32[]{:S(2)}) %all-to-all-start.2) | async-done | bytes 3145760 | tf_op jit(solution)/shard_map/all_to_all | solution.py:77
  102.4 3.6 all-to-all-start
  106.5 7.4 %fusion.1 = f32[384,768]{1,0:T(8,128)} fusion(bf16[384,4096]{1,0:T(8,128)(2,1)} %bitcast.12, bf16[1,768,4096]{2,1,0:T(8,128)(2,1)} %param.12), kind=kOutput, calls=%fused_computation.12 | convolution fusion | flops 2415919104 | bytes 10616832 | tf_op jit(solution)/shard_map/dot_general | solution.py:85
  113.8 63.1 %all-to-all-done = bf16[8,48,4096]{2,1,0:T(8,128)(2,1)S(1)} async-done(((bf16[8,48,4096]{2,1,0:T(8,128)(2,1)}), bf16[8,48,4096]{2,1,0:T(8,128)(2,1)S(1)}, u32[]{:S(2)}, u32[]{:S(2)}) %all-to-all-start) | async-done | bytes 3145760 | tf_op jit(solution)/shard_map/all_to_all | solution.py:51
  176.9 5.5 %fusion.7 = f32[384,768]{1,0:T(8,128)S(1)} fusion(bf16[384,4096]{1,0:T(8,128)(2,1)S(1)} %bitcast.95, bf16[1,4096,768]{2,1,0:T(8,128)(2,1)} %param.11), kind=kOutput, calls=%fused_computation.18 | convolution fusion | flops 2415919104 | bytes 10616832 | tf_op jit(solution)/shard_map/dot_general | solution.py:55
  182.4 6.8 %multiply_convert_fusion.1 = (bf16[384,768]{1,0:T(8,128)(2,1)}, bf16[384,768]{1,0:T(8,128)(2,1)}, bf16[384,768]{1,0:T(8,128)(2,1)S(1)}) fusion(f32[384,768]{1,0:T(8,128)S(1)} %copy-done.7, f32[384,768]{1,0:T(8,128)S(1)} %fusion.7, bf16[384,4096]{1,0:T(8,128)(2,1)S(1)} %bitcast.96, bf16[1,4096,768]{2,1,0:T(8,128)(2,1)} %param.10), kind=kOutput, calls=%fused_computation.29 | convolution fusion | flops 2420342784 | bytes 13565952 | tf_op jit(solution)/shard_map/dot_general | solution.py:54
  190.0 8.0 %convolution_convert_fusion = bf16[4096,768]{1,0:T(8,128)(2,1)} fusion(bf16[384,4096]{1,0:T(8,128)(2,1)} %bitcast.12, bf16[384,768]{1,0:T(8,128)(2,1)S(1)} %get-tuple-element.27), kind=kOutput, calls=%fused_computation.7 | convolution fusion | flops 2419064832 | bytes 10027008 | tf_op jit(solution)/shard_map/dot_general | solution.py:135
  198.1 6.4 %convolution_convert_fusion.2 = bf16[4096,768]{1,0:T(8,128)(2,1)} fusion(bf16[384,4096]{1,0:T(8,128)(2,1)S(1)} %bitcast.97, bf16[384,768]{1,0:T(8,128)(2,1)} %get-tuple-element.25), kind=kOutput, calls=%fused_computation.9 | convolution fusion | flops 2419064832 | bytes 10027008 | tf_op jit(solution)/shard_map/dot_general | solution.py:116
  204.5 12.3 %reduce-scatter.6.cloned.1.call-start = ((), (), s32[]{:S(2)}) async-start(), calls=%async_computation.7 | async-start | bytes 7864320 | tf_op jit(solution)/shard_map/reduce_scatter | solution.py:124
  216.8 6.4 %convolution_convert_fusion.1 = bf16[4096,768]{1,0:T(8,128)(2,1)} fusion(bf16[384,4096]{1,0:T(8,128)(2,1)S(1)} %bitcast.98, bf16[384,768]{1,0:T(8,128)(2,1)} %get-tuple-element.26), kind=kOutput, calls=%fused_computation.8 | convolution fusion | flops 2419064832 | bytes 10027008 | tf_op jit(solution)/shard_map/dot_general | solution.py:125
  224.3 9.0 %fusion.5 = f32[384,4096]{1,0:T(8,128)} fusion(bf16[384,768]{1,0:T(8,128)(2,1)S(1)} %copy-done.3, bf16[1,4096,768]{2,1,0:T(8,128)(2,1)} %param.11), kind=kOutput, calls=%fused_computation.16 | convolution fusion | flops 2415919104 | bytes 13172736 | tf_op jit(solution)/shard_map/dot_general | solution.py:95
  233.3 5.0 %add_convert_fusion = bf16[384,4096]{1,0:T(8,128)(2,1)S(1)} fusion(f32[384,4096]{1,0:T(8,128)} %fusion.5, bf16[384,768]{1,0:T(8,128)(2,1)S(1)} %copy-done.6, bf16[1,4096,768]{2,1,0:T(8,128)(2,1)S(1)} %bitcast.105), kind=kOutput, calls=%fused_computation.24 | convolution fusion | flops 2419064832 | bytes 16318464 | tf_op jit(solution)/shard_map/dot_general | solution.py:92
  241.5 4.0 fusion.15
  245.5 3.8 all-to-all-start.1
  249.3 4.7 %collective-permute-start.6 = (bf16[1,48,4096]{2,1,0:T(8,128)(2,1)}, bf16[1,48,4096]{2,1,0:T(8,128)(2,1)S(1)}, u32[]{:S(2)}, u32[]{:S(2)}) collective-permute-start(bf16[1,48,4096]{2,1,0:T(8,128)(2,1)} %get-tuple-element.17), channel_id=1, source_target_pairs={{0,7},{1,6},{2,5},{3,4},{4,3},{5,2},{6,1},{7,0},{8,15},{9,14},{10,... | collective-permute-start | bytes 1179656 | tf_op jit(solution)/shard_map/ppermute | solution.py:105
  260.2 82.8 %collective-permute-done.1 = bf16[1,48,4096]{2,1,0:T(8,128)(2,1)S(1)} collective-permute-done((bf16[1,48,4096]{2,1,0:T(8,128)(2,1)}, bf16[1,48,4096]{2,1,0:T(8,128)(2,1)S(1)}, u32[]{:S(2)}, u32[]{:S(2)}) %collective-permute-start.1) | collective-permute-done | bytes 393248 | tf_op jit(solution)/shard_map/ppermute | solution.py:105
  343.0 3.2 collective-permute-start.2
  347.0 15.1 %collective-permute-done.2 = bf16[1,48,4096]{2,1,0:T(8,128)(2,1)S(1)} collective-permute-done((bf16[1,48,4096]{2,1,0:T(8,128)(2,1)}, bf16[1,48,4096]{2,1,0:T(8,128)(2,1)S(1)}, u32[]{:S(2)}, u32[]{:S(2)}) %collective-permute-start.2) | collective-permute-done | bytes 393248 | tf_op jit(solution)/shard_map/ppermute | solution.py:105
  362.9 26.0 %collective-permute-done.3 = bf16[1,48,4096]{2,1,0:T(8,128)(2,1)S(1)} collective-permute-done((bf16[1,48,4096]{2,1,0:T(8,128)(2,1)}, bf16[1,48,4096]{2,1,0:T(8,128)(2,1)S(1)}, u32[]{:S(2)}, u32[]{:S(2)}) %collective-permute-start.3) | collective-permute-done | bytes 393248 | tf_op jit(solution)/shard_map/ppermute | solution.py:105
  392.0 4.4 gather_fusion.4
  396.4 7.5 %gather_fusion.5 = bf16[256,4096]{1,0:T(8,128)(2,1)} fusion(bf16[384,4096]{1,0:T(8,128)(2,1)} %bitcast.90, s32[1024]{0:T(1024)S(1)} %pad_clamp_fusion.2), kind=kCustom, calls=%fused_computation.5 | custom fusion | bytes 4195328 | tf_op jit(solution)/shard_map/gather | solution.py:109
  403.9 4.4 gather.29
  408.4 7.7 %reduce_sum.35 = bf16[128,4096]{1,0:T(8,128)(2,1)} reduce(bf16[128,2,4096]{2,1,0:T(2,128)(2,1)} %gather.29, bf16[]{:T(256)} %constant.17.clone.1), dimensions={1}, to_apply=%region_5.6 | reduce | flops 524288 | bytes 3145730 | tf_op jit(solution)/shard_map/reduce_sum | solution.py:110
  416.1 3.2 gather_fusion.1
  419.3 5.6 %reshape.126 = f32[128,2,4096]{2,1,0:T(2,128)} reshape(bf16[256,4096]{1,0:T(8,128)(2,1)} %gather_fusion.1) | data formatting | bytes 6291456 | tf_op jit(solution)/shard_map/convert_element_type | solution.py:69
  424.8 9.6 %multiply_reduce_fusion = bf16[128,4096]{1,0:T(8,128)(2,1)} fusion(f32[128,2,4096]{2,1,0:T(2,128)} %reshape.126, f32[128,2]{1,0:T(8,128)S(1)} %copy.14), kind=kLoop, calls=%fused_computation.26 | loop fusion | flops 1572864 | bytes 5243904 | tf_op jit(solution)/shard_map/reduce_sum | solution.py:71
  (79 shorter events, 24.5 us)
Async XLA Ops:
  7.2 8.4 %copy-start = (bf16[128,4096]{1,0:T(8,128)(2,1)S(1)}, bf16[128,4096]{1,0:T(8,128)(2,1)}, u32[]{:S(2)}) copy-start(bf16[128,4096]{1,0:T(8,128)(2,1)} %param.13) | copy-start | bytes 3145732
  24.1 7.5 %copy-start.2 = (bf16[128,4096]{1,0:T(8,128)(2,1)S(1)}, bf16[128,4096]{1,0:T(8,128)(2,1)}, u32[]{:S(2)}) copy-start(bf16[128,4096]{1,0:T(8,128)(2,1)} %param.7) | copy-start | bytes 3145732
  24.1 78.2 %all-to-all-start.2 = ((bf16[8,48,4096]{2,1,0:T(8,128)(2,1)}), bf16[8,48,4096]{2,1,0:T(8,128)(2,1)}, u32[]{:S(2)}, u32[]{:S(2)}) async-start(bf16[8,48,4096]{2,1,0:T(8,128)(2,1)} %fusion), calls=%async_computation.2 | async-start | bytes 6291456 | tf_op jit(solution)/shard_map/all_to_all | solution.py:77
  102.4 74.5 %all-to-all-start = ((bf16[8,48,4096]{2,1,0:T(8,128)(2,1)}), bf16[8,48,4096]{2,1,0:T(8,128)(2,1)S(1)}, u32[]{:S(2)}, u32[]{:S(2)}) async-start(bf16[8,48,4096]{2,1,0:T(8,128)(2,1)} %broadcast_select_fusion), calls=%async_computation | async-start | bytes 6291456 | tf_op jit(solution)/shard_map/all_to_all | solution.py:51
  106.0 328.4 %reduce-scatter.8.cloned.1.call-start = ((), (), s32[]{:S(2)}) async-start(), calls=%async_computation.8 | async-start | bytes 7864320 | tf_op jit(solution)/shard_map/reduce_scatter | solution.py:134
  176.9 5.5 %copy-start.7 = (f32[384,768]{1,0:T(8,128)S(1)}, f32[384,768]{1,0:T(8,128)}, u32[]{:S(2)}) copy-start(f32[384,768]{1,0:T(8,128)} %fusion.1) | copy-start | bytes 3538948
  189.1 0.8 copy-start.4
  198.0 239.0 %reduce-scatter.4.cloned.1.call-start = ((), (), s32[]{:S(2)}) async-start(), calls=%async_computation.6 | async-start | bytes 7864320 | tf_op jit(solution)/shard_map/reduce_scatter | solution.py:115
  204.5 232.5 %reduce-scatter.6.cloned.1.call-start = ((), (), s32[]{:S(2)}) async-start(), calls=%async_computation.7 | async-start | bytes 7864320 | tf_op jit(solution)/shard_map/reduce_scatter | solution.py:124
  223.2 1.1 copy-start.3
  223.2 10.0 %slice-start = ((s8[6291456]{0:T(1024)(128)(4,1)}), s8[2097152]{0:T(1024)(128)(4,1)S(1)}, s32[]{:S(2)}) async-start(s8[6291456]{0:T(1024)(128)(4,1)} %bitcast.104), calls=%async_computation.9 | async-start | bytes 4194304
  224.3 9.0 %slice-start.1 = ((s8[6291456]{0:T(1024)(128)(4,1)}), s8[4194304]{0:T(1024)(128)(4,1)S(1)}, s32[]{:S(2)}) async-start(s8[6291456]{0:T(1024)(128)(4,1)} %bitcast.104), calls=%async_computation.10 | async-start | bytes 8388608
  224.3 9.0 %copy-start.6 = (bf16[384,768]{1,0:T(8,128)(2,1)S(1)}, bf16[384,768]{1,0:T(8,128)(2,1)}, u32[]{:S(2)}) copy-start(bf16[384,768]{1,0:T(8,128)(2,1)} %get-tuple-element.25) | copy-start | bytes 1769476
  224.3 17.2 %slice-start.2 = ((s8[6291456]{0:T(1024)(128)(4,1)}), s8[4194304]{0:T(1024)(128)(4,1)S(1)}, s32[]{:S(2)}) async-start(s8[6291456]{0:T(1024)(128)(4,1)} %bitcast.106), calls=%async_computation.11 | async-start | bytes 8388608
  233.3 8.2 %slice-start.3 = ((s8[6291456]{0:T(1024)(128)(4,1)}), s8[2097152]{0:T(1024)(128)(4,1)S(1)}, s32[]{:S(2)}) async-start(s8[6291456]{0:T(1024)(128)(4,1)} %bitcast.106), calls=%async_computation.12 | async-start | bytes 4194304
  238.3 3.2 copy-start.5
  240.0 17.0 %collective-permute-start = (bf16[1,48,4096]{2,1,0:T(8,128)(2,1)}, bf16[1,48,4096]{2,1,0:T(8,128)(2,1)}, u32[]{:S(2)}, u32[]{:S(2)}) collective-permute-start(bf16[1,48,4096]{2,1,0:T(8,128)(2,1)} %get-tuple-element.23), channel_id=1, source_target_pairs={{0,1},{1,0},{2,3},{3,2},{4,5},{5,4},{6,7},{7,6},{8,9},{9,8},{10,11... | collective-permute-start | bytes 1179656 | tf_op jit(solution)/shard_map/ppermute | solution.py:105
  245.5 170.5 %all-to-all-start.1 = ((bf16[8,48,4096]{2,1,0:T(8,128)(2,1)}), bf16[8,48,4096]{2,1,0:T(8,128)(2,1)S(1)}, u32[]{:S(2)}, u32[]{:S(2)}) async-start(bf16[8,48,4096]{2,1,0:T(8,128)(2,1)} %bitcast.94), calls=%async_computation.1 | async-start | bytes 6291456 | tf_op jit(solution)/shard_map/all_to_all | solution.py:61
  249.3 141.9 %collective-permute-start.6 = (bf16[1,48,4096]{2,1,0:T(8,128)(2,1)}, bf16[1,48,4096]{2,1,0:T(8,128)(2,1)S(1)}, u32[]{:S(2)}, u32[]{:S(2)}) collective-permute-start(bf16[1,48,4096]{2,1,0:T(8,128)(2,1)} %get-tuple-element.17), channel_id=1, source_target_pairs={{0,7},{1,6},{2,5},{3,4},{4,3},{5,2},{6,1},{7,0},{8,15},{9,14},{10,... | collective-permute-start | bytes 1179656 | tf_op jit(solution)/shard_map/ppermute | solution.py:105
  254.1 136.4 %collective-permute-start.5 = (bf16[1,48,4096]{2,1,0:T(8,128)(2,1)}, bf16[1,48,4096]{2,1,0:T(8,128)(2,1)S(1)}, u32[]{:S(2)}, u32[]{:S(2)}) collective-permute-start(bf16[1,48,4096]{2,1,0:T(8,128)(2,1)} %get-tuple-element.18), channel_id=1, source_target_pairs={{0,6},{1,7},{2,4},{3,5},{4,2},{5,3},{6,0},{7,1},{8,14},{9,15},{10,... | collective-permute-start | bytes 1179656 | tf_op jit(solution)/shard_map/ppermute | solution.py:105
  254.6 135.0 %collective-permute-start.4 = (bf16[1,48,4096]{2,1,0:T(8,128)(2,1)}, bf16[1,48,4096]{2,1,0:T(8,128)(2,1)S(1)}, u32[]{:S(2)}, u32[]{:S(2)}) collective-permute-start(bf16[1,48,4096]{2,1,0:T(8,128)(2,1)} %get-tuple-element.19), channel_id=1, source_target_pairs={{0,5},{1,4},{2,7},{3,6},{4,1},{5,0},{6,3},{7,2},{8,13},{9,12},{10,... | collective-permute-start | bytes 1179656 | tf_op jit(solution)/shard_map/ppermute | solution.py:105
  255.2 133.7 %collective-permute-start.3 = (bf16[1,48,4096]{2,1,0:T(8,128)(2,1)}, bf16[1,48,4096]{2,1,0:T(8,128)(2,1)S(1)}, u32[]{:S(2)}, u32[]{:S(2)}) collective-permute-start(bf16[1,48,4096]{2,1,0:T(8,128)(2,1)} %get-tuple-element.20), channel_id=1, source_target_pairs={{0,4},{1,5},{2,6},{3,7},{4,0},{5,1},{6,2},{7,3},{8,12},{9,13},{10,... | collective-permute-start | bytes 1179656 | tf_op jit(solution)/shard_map/ppermute | solution.py:105
  257.0 86.0 %collective-permute-start.1 = (bf16[1,48,4096]{2,1,0:T(8,128)(2,1)}, bf16[1,48,4096]{2,1,0:T(8,128)(2,1)S(1)}, u32[]{:S(2)}, u32[]{:S(2)}) collective-permute-start(bf16[1,48,4096]{2,1,0:T(8,128)(2,1)} %get-tuple-element.22), channel_id=1, source_target_pairs={{0,2},{1,3},{2,0},{3,1},{4,6},{5,7},{6,4},{7,5},{8,10},{9,11},{10,... | collective-permute-start | bytes 1179656 | tf_op jit(solution)/shard_map/ppermute | solution.py:105
  343.0 19.1 %collective-permute-start.2 = (bf16[1,48,4096]{2,1,0:T(8,128)(2,1)}, bf16[1,48,4096]{2,1,0:T(8,128)(2,1)S(1)}, u32[]{:S(2)}, u32[]{:S(2)}) collective-permute-start(bf16[1,48,4096]{2,1,0:T(8,128)(2,1)} %get-tuple-element.21), channel_id=1, source_target_pairs={{0,3},{1,2},{2,1},{3,0},{4,7},{5,6},{6,5},{7,4},{8,11},{9,10},{10,... | collective-permute-start | bytes 1179656 | tf_op jit(solution)/shard_map/ppermute | solution.py:105
  419.3 17.8 %copy-start.1 = (bf16[128,4096]{1,0:T(8,128)(2,1)S(1)}, bf16[128,4096]{1,0:T(8,128)(2,1)}, u32[]{:S(2)}) copy-start(bf16[128,4096]{1,0:T(8,128)(2,1)} %param.13) | copy-start | bytes 3145732
Sparse Core Ops, SparseCore 0:
  198.1 57.4 reduce-scatter.7
  258.9 58.3 reduce-scatter.3
  320.4 58.3 reduce-scatter.5
